TPU v7x, 32 devices: a whole 2x2x4 slice. The times are simulated.
32 devices in a mesh: groups: 2 (over y), dp: 4 (over z), rep: 4 (over x, core).
Axes of the slice: x: 2, y: 2, z: 4, core: 2. Of those that a mesh axis runs over, the one named last changes fastest.
Arguments:
- latent_store: bfloat16 [8, 48, 576, 128], P(('groups', 'dp'), 'rep'), parts along dimension 0, may hold values from -6 to 6
- page_rank: int32 [8, 48], P('groups', 'rep'), parts along dimension 0, may hold values from 0 to 3, as said below
- page_index: int32 [8, 48], P('groups', 'rep'), parts along dimension 0, may hold values from 0 to 11, as said below
- lengths: int32 [8, 1], P('groups'), parts along dimension 0, may hold values from 1536 to 6144, as said below
- queries: bfloat16 [16, 36864], P(('groups', 'dp')), parts along dimension 0, may hold values from -250 to 250
- new_latent: bfloat16 [16, 576], P(('groups', 'dp')), parts along dimension 0, may hold values from -4 to 4
- up_value: bfloat16 [64, 512, 128], P('dp'), may hold values from -0.25 to 0.25
- out_proj: bfloat16 [8192, 7168], P('dp', 'rep'), may hold values from -0.0625 to 0.0625
- residual: bfloat16 [16, 7168], P(('groups', 'dp'), 'rep'), parts along dimension 0, may hold values from -11 to 11
- norm_gain: float32 [7168], P('rep'), may hold values from 0.1 to 1.9
- w_gate: bfloat16 [7168, 12288], P('rep', 'dp'), may hold values from -0.0625 to 0.0625
- w_up: bfloat16 [7168, 12288], P('rep', 'dp'), may hold values from -0.0625 to 0.0625
- w_down: bfloat16 [12288, 7168], P('dp', 'rep'), may hold values from -0.0546875 to 0.0546875
Outputs:
- layer_out: bfloat16 [16, 7168], P(('groups', 'dp'), 'rep'), parts along dimension 0
There are 2 independent parts, one for each index of `groups`. A program takes and returns all parts, laid end to end along the dimension named above; an argument that names none is the same for every part. Nothing has to cross between parts.
Inputs may be any that keep to these rules, and one draw needn't show every extreme that they name: page_rank[d, q] is the storage rank holding slot q of rank d, on its device with rep index q // 12; one storage device holds at most 3 slot of one rank, and some holds exactly 3. page_index[d, q] is the slot's page among the 12 pages of its storage device; over all ranks every page of every storage device is named by exactly one slot. `lengths`: some request has exactly 6144 tokens.
All inputs are finite; a program needn't handle non-finite values.
Results may differ from a plain program's by a relative error of at most 0.015.
Values may be sent and summed in bfloat16 or wider, within the bound.
No kernel may reach another device: no remote copies, remote signals or barrier semaphores. Data moves between devices by JAX's collectives and lax.ppermute only.
A program may use at most 128 MiB of HBM per device.

v0:
```python
import math
import jax
import jax.numpy as jnp
from jax import lax
from jax.sharding import PartitionSpec as P

D = 7168
CKV = 512
PAGE = 128
PAGES = 48
score_scale = 1.0 / math.sqrt(192.0)
epsilon = 1e-06
mask_value = -1e30


def merged_2(array, axis, join):
    gathered = jax.tree.map(
        lambda a, kind: lax.all_gather(a.astype(kind), axis),
        array,
        jax.tree.map(lambda a: jnp.bfloat16 if a.dtype == jnp.float32 else a.dtype, array),
    )

    def take(source):
        return jax.tree.map(
            lambda a, own: lax.dynamic_index_in_dim(a, source, 0, False).astype(own.dtype),
            gathered,
            array,
        )

    return lax.fori_loop(
        1, lax.axis_size(axis), lambda source, state: join(state, take(source)), take(0)
    )


def page_partials(page_keys, page_queries, key_counts):
    scores = (
        jnp.einsum("pshl,plt->psht", page_queries, page_keys, preferred_element_type=jnp.float32)
        * score_scale
    )
    places = lax.broadcasted_iota(jnp.int32, scores.shape, 3)
    visible = places < key_counts[:, None, None, None]
    scores = jnp.where(visible, scores, mask_value)
    row_peak = jnp.max(scores, axis=3)
    weights = jnp.where(visible, jnp.exp(scores - row_peak[..., None]), 0.0)
    row_total = jnp.sum(weights, axis=3)
    partial_value = jnp.einsum(
        "psht,pct->pshc",
        weights.astype(jnp.bfloat16),
        page_keys[:, :CKV, :],
        preferred_element_type=jnp.float32,
    )
    return (partial_value, row_peak, row_total)


def join_pages(partial_value, row_peak, row_total, slot_request, requests):
    owner_mask = slot_request[None, :] == jnp.arange(requests, dtype=jnp.int32)[:, None]
    spread = owner_mask[:, :, None, None]
    best_peak = jnp.max(jnp.where(spread, row_peak[None], mask_value), axis=1)
    factor = jnp.where(spread, jnp.exp(row_peak[None] - best_peak[:, None]), 0.0)
    joined = jnp.einsum("jpsh,pshc->jshc", factor, partial_value, precision=lax.Precision.HIGHEST)
    summed = jnp.sum(factor * row_total[None], axis=1)
    return (joined, best_peak, summed)


def combine(former, latter):
    former_sum, former_peak, former_total = former
    latter_sum, latter_peak, latter_total = latter
    highest = jnp.maximum(former_peak, latter_peak)
    former_scale = jnp.exp(former_peak - highest)
    latter_scale = jnp.exp(latter_peak - highest)
    merged_sum = former_sum * former_scale[..., None] + latter_sum * latter_scale[..., None]
    return (merged_sum, highest, former_total * former_scale + latter_total * latter_scale)


def fresh_partial(query_rows, fresh_rows, active):
    scores = (
        jnp.einsum("jshl,jul->jshu", query_rows, fresh_rows, preferred_element_type=jnp.float32)
        * score_scale
    )
    step_query = lax.broadcasted_iota(jnp.int32, scores.shape, 1)
    step_key = lax.broadcasted_iota(jnp.int32, scores.shape, 3)
    visible = (step_key <= step_query) & active
    scores = jnp.where(visible, scores, mask_value)
    row_peak = jnp.max(scores, axis=3)
    weights = jnp.where(visible, jnp.exp(scores - row_peak[..., None]), 0.0)
    row_total = jnp.sum(weights, axis=3)
    partial_value = jnp.einsum(
        "jshu,juc->jshc",
        weights.astype(jnp.bfloat16),
        fresh_rows[:, :, :CKV],
        preferred_element_type=jnp.float32,
    )
    return (partial_value, row_peak, row_total)


def on_device(
    latent_store,
    page_rank,
    page_index,
    lengths,
    queries,
    new_latent,
    up_value,
    out_proj,
    residual,
    norm_gain,
    w_gate,
    w_up,
    w_down,
):
    my_rank = lax.axis_index("dp")
    my_column = lax.axis_index("rep")
    rank_count, slot_count = page_rank.shape
    capacity = (slot_count + rank_count - 1) // rank_count
    requests = lengths.shape[1]
    rows_here = residual.shape[0]
    steps_count = rows_here // requests
    latent_width = new_latent.shape[1]
    head_count = queries.shape[1] // latent_width
    query_rows = queries.reshape(requests, steps_count, head_count, latent_width)
    fresh_rows = new_latent.reshape(requests, steps_count, latent_width)
    slot_order = jnp.arange(slot_count, dtype=jnp.int32)
    request_ids = jnp.arange(requests, dtype=jnp.int32)
    cap_ids = jnp.arange(capacity, dtype=jnp.int32)
    global_slot = my_column * slot_count + slot_order
    slot_request = global_slot // PAGES
    slot_page = global_slot % PAGES
    own_lengths = lax.dynamic_index_in_dim(lengths, my_rank, 0, keepdims=False)
    slot_length = jnp.sum(
        jnp.where(slot_request[:, None] == request_ids[None, :], own_lengths[None, :], 0), axis=1
    )
    key_counts = jnp.clip(slot_length - slot_page * PAGE, 0, PAGE)
    my_sources = lax.dynamic_index_in_dim(page_rank, my_rank, 0, keepdims=False)
    earlier = (my_sources[None, :] == my_sources[:, None]) & (
        slot_order[None, :] < slot_order[:, None]
    )
    arrival_rank = jnp.sum(earlier.astype(jnp.int32), axis=1)
    arrival_slot = my_sources * capacity + arrival_rank
    held_here = page_rank == my_rank
    held_order = jnp.cumsum(held_here.astype(jnp.int32), axis=1) - 1
    selector = held_here[:, None, :] & (held_order[:, None, :] == cap_ids[None, :, None])
    sent_valid = jnp.any(selector, axis=2).reshape(-1)
    sent_page = jnp.sum(jnp.where(selector, page_index[:, None, :], 0), axis=2).reshape(-1)
    stored = latent_store[0]
    outgoing = jnp.take(stored, sent_page, axis=0)
    outgoing = jnp.where(sent_valid[:, None, None], outgoing, jnp.zeros_like(outgoing))
    arrived = lax.all_to_all(outgoing, "dp", split_axis=0, concat_axis=0, tiled=True)
    restored = jnp.take(arrived, arrival_slot, axis=0)
    page_queries = jnp.take(query_rows, slot_request, axis=0)
    partial_value, row_peak, row_total = page_partials(restored, page_queries, key_counts)
    joined = join_pages(partial_value, row_peak, row_total, slot_request, requests)
    local_part = combine(joined, fresh_partial(query_rows, fresh_rows, my_column == 0))
    merged = merged_2(local_part, "rep", combine)
    attention = (
        (merged[0] / merged[2][..., None]).astype(jnp.bfloat16).reshape(rows_here, head_count, CKV)
    )
    headed = lax.all_to_all(attention, "dp", split_axis=1, concat_axis=0, tiled=True)
    values = jnp.einsum("rhc,hcv->rhv", headed, up_value, preferred_element_type=jnp.float32)
    values = values.astype(jnp.bfloat16).reshape(headed.shape[0], -1)
    picked = values
    attn_out = lax.psum_scatter(
        jnp.dot(picked, out_proj, preferred_element_type=jnp.float32).astype(jnp.bfloat16),
        "dp",
        scatter_dimension=0,
        tiled=True,
    ).astype(jnp.float32)
    mixed_rows = residual.astype(jnp.float32) + attn_out
    squares = lax.psum(jnp.sum(mixed_rows * mixed_rows, axis=1), "rep")
    normed = (mixed_rows * lax.rsqrt(squares / D + epsilon)[:, None] * norm_gain).astype(
        jnp.bfloat16
    )
    piece = lax.all_gather(normed, "dp", axis=0, tiled=True)
    gate_part = jnp.dot(piece, w_gate, preferred_element_type=jnp.float32)
    up_part = jnp.dot(piece, w_up, preferred_element_type=jnp.float32)
    partial_rows = jnp.concatenate([gate_part, up_part], axis=1)
    gate_up = lax.psum(partial_rows.astype(jnp.bfloat16), "rep").astype(jnp.float32)
    hidden_width = w_gate.shape[1]
    hidden = (jax.nn.silu(gate_up[:, :hidden_width]) * gate_up[:, hidden_width:]).astype(
        jnp.bfloat16
    )
    picked = hidden
    mlp_out = lax.psum_scatter(
        jnp.dot(picked, w_down, preferred_element_type=jnp.float32).astype(jnp.bfloat16),
        "dp",
        scatter_dimension=0,
        tiled=True,
    ).astype(jnp.float32)
    return (mixed_rows + mlp_out).astype(jnp.bfloat16)


def solution(mesh):
    in_specs = (
        P(("groups", "dp"), "rep", None, None),
        P("groups", "rep"),
        P("groups", "rep"),
        P("groups", None),
        P(("groups", "dp"), None),
        P(("groups", "dp"), None),
        P("dp", None, None),
        P("dp", "rep"),
        P(("groups", "dp"), "rep"),
        P("rep"),
        P("rep", "dp"),
        P("rep", "dp"),
        P("dp", "rep"),
    )
    out_specs = P(("groups", "dp"), "rep")
    return jax.shard_map(
        on_device, mesh=mesh, in_specs=in_specs, out_specs=out_specs, check_vma=False
    )
```

profile of v0, /device:TPU:0, one launch (start us, length us, event | category | flops | bytes accessed | tf_op | source)
XLA Modules:
  0.0 225.6 jit_solution(1305932446610789168)
XLA Ops:
  6.5 0.8 fusion.66
  7.4 0.2 reduce_window_sum.11
  7.6 0.1 fusion.45
  7.7 0.8 select_reduce_fusion.1
  8.5 0.1 copy.21
  8.8 0.1 copy.20
  9.0 3.5 %gather_fusion = bf16[12,576,128]{2,1,0:T(8,128)(2,1)} fusion(bf16[12,576,128]{2,1,0:T(8,128)(2,1)} %bitcast.145, s32[1024]{0:T(1024)S(1)} %pad_clamp_fusion.1), kind=kCustom, calls=%fused_computation.clone | custom fusion | bytes 3538992 | tf_op jit(solution)/shard_map/jit(_take)/gather | solution.py:145
  12.5 2.9 %select_select_fusion = bf16[12,576,128]{2,1,0:T(8,128)(2,1)} fusion(bf16[12,576,128]{2,1,0:T(8,128)(2,1)} %gather_fusion, pred[12]{0:T(512)(128)(4,1)S(1)} %get-tuple-element.237, pred[12]{0:T(512)(128)(4,1)S(1)} %broadcast_in_dim.122), kind=kLoop, calls=%fused_computation.26 | loop fusion | flops 1769472 | bytes 3538968 | tf_op jit(solution)/shard_map/jit(_where)/select_n | solution.py:146
  15.4 6.5 %all-to-all-start = ((bf16[12,576,128]{2,1,0:T(8,128)(2,1)}), bf16[12,576,128]{2,1,0:T(8,128)(2,1)}, u32[]{:S(2)}, u32[]{:S(2)}) async-start(bf16[12,576,128]{2,1,0:T(8,128)(2,1)} %select_select_fusion), calls=%async_computation | async-start | bytes 3538944 | tf_op jit(solution)/shard_map/all_to_all | solution.py:147
  21.9 0.2 reshape.402
  22.1 0.6 constant_dynamic-slice_fusion.3
  22.7 0.6 fusion.60
  23.3 0.2 convert_reduce_fusion
  23.5 0.2 fusion.68
  23.8 39.4 %all-to-all-done = bf16[12,576,128]{2,1,0:T(8,128)(2,1)} async-done(((bf16[12,576,128]{2,1,0:T(8,128)(2,1)}), bf16[12,576,128]{2,1,0:T(8,128)(2,1)}, u32[]{:S(2)}, u32[]{:S(2)}) %all-to-all-start) | async-done | bytes 1769504 | tf_op jit(solution)/shard_map/all_to_all | solution.py:147
  63.2 3.5 %gather_fusion.1 = bf16[12,576,128]{2,1,0:T(8,128)(2,1)} fusion(bf16[12,576,128]{2,1,0:T(8,128)(2,1)} %all-to-all-done, s32[1024]{0:T(1024)S(1)} %pad_clamp_fusion), kind=kCustom, calls=%fused_computation.1.clone | custom fusion | bytes 3538992 | tf_op jit(solution)/shard_map/jit(_take)/gather | solution.py:148
  66.7 1.7 broadcast_select_fusion
  68.4 0.8 fusion.67
  69.3 0.6 fusion.30
  69.8 2.3 %fusion.13 = f32[12,2,64,512]{3,2,1,0:T(8,128)} fusion(bf16[12,576,128]{2,1,0:T(8,128)(2,1)S(1)} %broadcast_select_fusion, f32[12,2,64,128]{3,2,1,0:T(8,128)S(1)} %get-tuple-element.233, f32[12,2,64]{2,1,0:T(2,128)S(1)} %get-tuple-element.232, s32[12]{0:T(128)S(1)} %fusion.60), kind=kOutput, calls=%fused_computation.29 | convolution fusion | flops 202113024 | bytes 5517824 | tf_op jit(solution)/shard_map/psht,pct->pshc/dot_general | solution.py:46
  72.4 5.1 %all_gather.20 = bf16[4,1,2,64]{3,2,1,0:T(2,128)(2,1)S(1)} all-gather(bf16[1,1,2,64]{3,2,1,0:T(2,128)(2,1)S(1)} %fusion.50), channel_id=1, replica_groups=mesh['groups'=2,'dp'=4,'rep'=4] {'rep'}, dimensions={0}, use_global_device_ids=true | all-gather | bytes 1280 | tf_op jit(solution)/shard_map/all_gather | solution.py:18
  77.4 0.1 copy.29
  77.5 7.4 %fusion.7 = f32[2,64,1,512]{3,2,1,0:T(1,128)S(1)} fusion(f32[12,2,64,1]{0,3,2,1:T(1,128)S(1)} %copy.29, f32[12,2,64,512]{3,2,1,0:T(8,128)} %fusion.13), kind=kOutput, calls=%fused_computation.16 | convolution fusion | flops 9437184 | bytes 3414016 | tf_op jit(solution)/shard_map/jpsh,pshc->jshc/dot_general | solution.py:60
  84.9 0.2 fusion.25
  85.2 7.3 %all-gather = bf16[8,64,512]{2,1,0:T(8,128)(2,1)S(1)} all-gather(bf16[2,64,512]{2,1,0:T(8,128)(2,1)S(1)} %fusion.25), channel_id=2, replica_groups=mesh['groups'=2,'dp'=4,'rep'=4] {'rep'}, dimensions={0}, use_global_device_ids=true | all-gather | bytes 655360 | tf_op jit(solution)/shard_map/all_gather | solution.py:18
  92.5 5.1 %all_gather.19 = bf16[4,1,2,64]{3,2,1,0:T(2,128)(2,1)S(1)} all-gather(bf16[1,1,2,64]{3,2,1,0:T(2,128)(2,1)S(1)} %fusion.54), channel_id=1, replica_groups=mesh['groups'=2,'dp'=4,'rep'=4] {'rep'}, dimensions={0}, use_global_device_ids=true | all-gather | bytes 1280 | tf_op jit(solution)/shard_map/all_gather | solution.py:18
  97.5 0.6 while.19
  97.6 0.1 fusion.84
  97.8 0.1 fusion.84
  98.0 0.1 fusion.84
  98.1 0.1 copy.23
  98.2 1.0 fusion.38
  99.2 3.3 %all-to-all-start.1 = ((bf16[2,64,512]{2,0,1:T(2,128)(2,1)}), bf16[2,64,512]{2,0,1:T(2,128)(2,1)S(1)}, u32[]{:S(2)}, u32[]{:S(2)}) async-start(bf16[2,64,512]{2,0,1:T(2,128)(2,1)} %fusion.38), calls=%async_computation.1 | async-start | bytes 262144 | tf_op jit(solution)/shard_map/all_to_all | solution.py:157
  102.6 0.6 dynamic-slice
  103.8 5.2 %all-to-all-done.1 = bf16[2,64,512]{2,0,1:T(2,128)(2,1)S(1)} async-done(((bf16[2,64,512]{2,0,1:T(2,128)(2,1)}), bf16[2,64,512]{2,0,1:T(2,128)(2,1)S(1)}, u32[]{:S(2)}, u32[]{:S(2)}) %all-to-all-start.1) | async-done | bytes 131104 | tf_op jit(solution)/shard_map/all_to_all | solution.py:157
  109.2 4.4 %convolution_convert_fusion.3 = bf16[8,1792]{1,0:T(8,128)(2,1)S(1)} fusion(bf16[2048,1792]{1,0:T(8,128)(2,1)} %param.24, bf16[8,16,512]{2,0,1:T(8,128)(2,1)S(1)} %all_to_all.20, bf16[16,512,128]{2,1,0:T(8,128)(2,1)S(1)} %copy-done), kind=kOutput, calls=%fused_computation.21 | convolution fusion | flops 75528192 | bytes 9596928 | tf_op jit(solution)/shard_map/dot_general | solution.py:162
  113.6 17.5 %all-reduce = bf16[8,1792]{1,0:T(8,128)(2,1)S(1)} all-reduce(bf16[8,1792]{1,0:T(8,128)(2,1)S(1)} %convolution_convert_fusion.3), channel_id=3, replica_groups=mesh['groups'=2,'dp'=4,'rep'=4] {'dp'}, use_global_device_ids=true, to_apply=%region_12.14.clone | all-reduce | flops 14336 | bytes 57344
  131.1 0.1 multiply_reduce_fusion
  131.2 5.8 %psum.14 = f32[2]{0:T(128)S(1)} all-reduce(f32[2]{0:T(128)S(1)} %multiply_reduce_fusion), channel_id=1, replica_groups=mesh['groups'=2,'dp'=4,'rep'=4] {'rep'}, use_global_device_ids=true, to_apply=%region_14.16 | all-reduce | flops 2 | bytes 16 | tf_op jit(solution)/shard_map/psum | solution.py:168
  137.1 13.2 %all-gather.1 = bf16[4,2,1792]{2,1,0:T(2,128)(2,1)S(1)} all-gather(bf16[1,2,1792]{2,1,0:T(2,128)(2,1)S(1)} %fusion.43), channel_id=1, replica_groups=mesh['groups'=2,'dp'=4,'rep'=4] {'dp'}, dimensions={0}, use_global_device_ids=true | all-gather | bytes 35840 | tf_op jit(solution)/shard_map/all_gather | solution.py:172
  150.3 5.7 %convolution_convert_fusion = bf16[8,3072]{1,0:T(8,128)(2,1)S(1)} fusion(bf16[8,1792]{1,0:T(8,128)(2,1)S(1)} %reshape.433, bf16[1792,3072]{1,0:T(8,128)(2,1)} %param.28), kind=kOutput, calls=%fused_computation.18 | convolution fusion | flops 88104960 | bytes 11087872 | tf_op jit(solution)/shard_map/dot_general | solution.py:174
  156.0 5.7 %convolution_convert_fusion.1 = bf16[8,3072]{1,0:T(8,128)(2,1)S(1)} fusion(bf16[8,1792]{1,0:T(8,128)(2,1)S(1)} %reshape.433, bf16[1792,3072]{1,0:T(8,128)(2,1)} %param.27), kind=kOutput, calls=%fused_computation.19 | convolution fusion | flops 88104960 | bytes 11087872 | tf_op jit(solution)/shard_map/dot_general | solution.py:173
  161.7 0.6 pad_maximum_fusion
  162.3 30.3 %all-reduce.4.cloned.1.call-done = bf16[8,6144]{1,0:T(8,128)(2,1)} async-done(((bf16[8,6144]{1,0:T(8,128)(2,1)}), bf16[8,6144]{1,0:T(8,128)(2,1)}) %all-reduce.4.cloned.1.call-update) | async-done | bytes 98320 | tf_op jit(solution)/shard_map/psum | solution.py:176
  192.6 0.9 convert_element_type.203
  193.5 5.7 %convolution_convert_fusion.2 = bf16[8,1792]{1,0:T(8,128)(2,1)S(1)} fusion(bf16[3072,1792]{1,0:T(8,128)(2,1)} %param.29, f32[8,6144]{1,0:T(8,128)S(1)} %convert_element_type.203), kind=kOutput, calls=%fused_computation.20 | convolution fusion | flops 88242176 | bytes 11235328 | tf_op jit(solution)/shard_map/dot_general | solution.py:183
  199.2 19.0 %all-reduce.1 = bf16[8,1792]{1,0:T(8,128)(2,1)S(1)} all-reduce(bf16[8,1792]{1,0:T(8,128)(2,1)S(1)} %convolution_convert_fusion.2), channel_id=4, replica_groups=mesh['groups'=2,'dp'=4,'rep'=4] {'dp'}, use_global_device_ids=true, to_apply=%region_16.18.clone | all-reduce | flops 14336 | bytes 57344
  218.2 0.6 add_convert_fusion
  (50 shorter events, 1.0 us)
Async XLA Ops:
  6.5 102.6 %copy-start = (bf16[16,512,128]{2,1,0:T(8,128)(2,1)S(1)}, bf16[16,512,128]{2,1,0:T(8,128)(2,1)}, u32[]{:S(2)}) copy-start(bf16[16,512,128]{2,1,0:T(8,128)(2,1)} %param.23) | copy-start | bytes 6291460
  15.4 6.5 %copy-start.1 = (bf16[2,36864]{1,0:T(2,128)(2,1)S(1)}, bf16[2,36864]{1,0:T(2,128)(2,1)}, u32[]{:S(2)}) copy-start(bf16[2,36864]{1,0:T(2,128)(2,1)} %param.21) | copy-start | bytes 442372
  15.4 6.7 %copy-start.6 = (s32[4,1]{0,1:T(1,128)S(1)}, s32[4,1]{0,1:T(1,128)}, u32[]{:S(2)}) copy-start(s32[4,1]{0,1:T(1,128)} %param.20) | copy-start | bytes 52
  15.4 7.3 %copy-start.5 = (s32[4,12]{1,0:T(4,128)S(1)}, s32[4,12]{1,0:T(4,128)}, u32[]{:S(2)}) copy-start(s32[4,12]{1,0:T(4,128)} %param.18) | copy-start | bytes 580
  15.4 8.1 %copy-start.3 = (bf16[2,576]{1,0:T(2,128)(2,1)S(1)}, bf16[2,576]{1,0:T(2,128)(2,1)}, u32[]{:S(2)}) copy-start(bf16[2,576]{1,0:T(2,128)(2,1)} %param.22) | copy-start | bytes 6916
  15.4 47.8 %all-to-all-start = ((bf16[12,576,128]{2,1,0:T(8,128)(2,1)}), bf16[12,576,128]{2,1,0:T(8,128)(2,1)}, u32[]{:S(2)}, u32[]{:S(2)}) async-start(bf16[12,576,128]{2,1,0:T(8,128)(2,1)} %select_select_fusion), calls=%async_computation | async-start | bytes 3538944 | tf_op jit(solution)/shard_map/all_to_all | solution.py:147
  97.5 5.0 %copy-start.7 = (u32[32]{0:T(128)S(1)}, u32[32]{0:T(128)}, u32[]{:S(2)}) copy-start(u32[32]{0:T(128)} %constant.150) | copy-start | bytes 388
  99.2 9.8 %all-to-all-start.1 = ((bf16[2,64,512]{2,0,1:T(2,128)(2,1)}), bf16[2,64,512]{2,0,1:T(2,128)(2,1)S(1)}, u32[]{:S(2)}, u32[]{:S(2)}) async-start(bf16[2,64,512]{2,0,1:T(2,128)(2,1)} %fusion.38), calls=%async_computation.1 | async-start | bytes 262144 | tf_op jit(solution)/shard_map/all_to_all | solution.py:157
  102.5 90.1 %all-reduce.4.cloned.1.call-start = ((), (), s32[]{:S(2)}) async-start(), calls=%async_computation.2 | async-start | bytes 196608 | tf_op jit(solution)/shard_map/psum | solution.py:176
  109.2 21.9 %copy-start.2 = (bf16[2,1792]{1,0:T(2,128)(2,1)S(1)}, bf16[2,1792]{1,0:T(2,128)(2,1)}, u32[]{:S(2)}) copy-start(bf16[2,1792]{1,0:T(2,128)(2,1)} %param.25) | copy-start | bytes 21508
  109.2 27.9 %copy-start.4 = (f32[1792]{0:T(1024)S(1)}, f32[1792]{0:T(1024)}, u32[]{:S(2)}) copy-start(f32[1792]{0:T(1024)} %param.26) | copy-start | bytes 21508
Sparse Core Ops, SparseCore 0:
  162.4 30.1 all-reduce.3
where the time goes:
time: 226 us
  waiting for transfers between devices  74.9 us (33%)
  blocking collectives  72.8 us (32%)
  matrix products  32.4 us (14%)
  between operations  14.3 us (6%)
  other arithmetic  12.1 us (5%)
  starting transfers between devices  9.85 us (4%)
  local copies, waits for them, and re-layouts  9.15 us (4%)
    all_to_all x1, waiting for transfers between devices, on_device(): lax.all_to_all(outgoing, 'dp', split_axis=0, concat_axis=0, tiled=True)  39.4 us
    unnamed x2, blocking collectives  36.4 us
    psum x1, waiting for transfers between devices, on_device(): lax.psum(partial_rows.astype(jnp.bfloat16), 'rep').astype(jnp.float32)  30.3 us
    all_gather x3, blocking collectives, merged_2(): lax.all_gather(a.astype(kind), axis)  17.4 us
    all_gather x1, blocking collectives, on_device(): piece = lax.all_gather(normed, 'dp', axis=0, tiled=True)  13.2 us
    dot_general x1, matrix products, join_pages(): jnp.einsum('jpsh,pshc->jshc', factor, partial_value, precision=lax.Precis...  7.4 us
    all_to_all x1, starting transfers between devices, on_device(): lax.all_to_all(outgoing, 'dp', split_axis=0, concat_axis=0, tiled=True)  6.49 us
    psum x1, blocking collectives, on_device(): squares = lax.psum(jnp.sum(mixed_rows * mixed_rows, axis=1), 'rep')  5.84 us
  transfers between devices with their start and end apart: 3, of which 3 were waited for; matrix products, arithmetic and copies ran while one was open for 1% of the time, Pallas kernels for 0%

commit v1 on v0

--- a/solution.py
+++ b/solution.py
@@ -173,7 +173,9 @@
     gate_part = jnp.dot(piece, w_gate, preferred_element_type=jnp.float32)
     up_part = jnp.dot(piece, w_up, preferred_element_type=jnp.float32)
     partial_rows = jnp.concatenate([gate_part, up_part], axis=1)
-    gate_up = lax.psum(partial_rows.astype(jnp.bfloat16), "rep").astype(jnp.float32)
+    gate_up = jnp.sum(lax.all_gather(partial_rows.astype(jnp.bfloat16), "rep"), axis=0).astype(
+        jnp.float32
+    )
     hidden_width = w_gate.shape[1]
     hidden = (jax.nn.silu(gate_up[:, :hidden_width]) * gate_up[:, hidden_width:]).astype(
         jnp.bfloat16

time: 226 us -> 185 us (0.82)
  waiting for transfers between devices: 74.9 us -> 44.6 us
  between operations: 14.3 us -> 0.89 us
  blocking collectives: 72.8 us -> 76.4 us
    psum x1 -> x0, waiting for transfers between devices: 30.3 us -> none  [on_device(): lax.psum(partial_rows.astype(jnp.bfloat16), 'rep').astype(jnp.float32)]
    all_gather x0 -> x1, blocking collectives: none -> 6.68 us  [on_device(): lax.all_gather(partial_rows.astype(jnp.bfloat16), 'rep')]
    unnamed x2, blocking collectives: 36.4 us -> 33.3 us
  transfers between devices with their start and end apart: 3 -> 2, of which waited for: 3 -> 2; matrix products, arithmetic and copies ran while one was open for 1% -> 1% of each run, Pallas kernels for 0% -> 0%
where the time goes in v1:
time: 185 us; the launch traced here: 184 us
  blocking collectives  76.4 us (41%)
  waiting for transfers between devices  44.6 us (24%)
  matrix products  32.4 us (18%)
  other arithmetic  10.7 us (6%)
  starting transfers between devices  9.81 us (5%)
  local copies, waits for them, and re-layouts  9.15 us (5%)
    all_to_all x1, waiting for transfers between devices, on_device(): lax.all_to_all(outgoing, 'dp', split_axis=0, concat_axis=0, tiled=True)  39.4 us
    unnamed x2, blocking collectives  33.3 us
    all_gather x3, blocking collectives, merged_2(): lax.all_gather(a.astype(kind), axis)  17.4 us
    all_gather x1, blocking collectives, on_device(): piece = lax.all_gather(normed, 'dp', axis=0, tiled=True)  13.4 us
    dot_general x1, matrix products, join_pages(): jnp.einsum('jpsh,pshc->jshc', factor, partial_value, precision=lax.Precis...  7.4 us
    all_gather x1, blocking collectives, on_device(): lax.all_gather(partial_rows.astype(jnp.bfloat16), 'rep')  6.68 us
    all_to_all x1, starting transfers between devices, on_device(): lax.all_to_all(outgoing, 'dp', split_axis=0, concat_axis=0, tiled=True)  6.49 us
    dot_general x1, matrix products, on_device(): gate_part = jnp.dot(piece, w_gate, preferred_element_type=jnp.float32)  5.66 us
  transfers between devices with their start and end apart: 2, of which 2 were waited for; matrix products, arithmetic and copies ran while one was open for 1% of the time, Pallas kernels for 0%

profile of v1, /device:TPU:0, one launch (start us, length us, event | category | flops | bytes accessed | tf_op | source)
XLA Modules:
  0.0 184.1 jit_solution(6700640061107649459)
XLA Ops:
  0.0 0.8 fusion.68
  0.8 0.2 reduce_window_sum.11
  1.0 0.1 fusion.47
  1.2 0.8 select_reduce_fusion.1
  2.0 0.1 copy.21
  2.2 0.1 copy.20
  2.4 3.5 %gather_fusion = bf16[12,576,128]{2,1,0:T(8,128)(2,1)} fusion(bf16[12,576,128]{2,1,0:T(8,128)(2,1)} %bitcast.149, s32[1024]{0:T(1024)S(1)} %pad_clamp_fusion.1), kind=kCustom, calls=%fused_computation.clone | custom fusion | bytes 3538992 | tf_op jit(solution)/shard_map/jit(_take)/gather | solution.py:145
  5.9 2.9 %select_select_fusion = bf16[12,576,128]{2,1,0:T(8,128)(2,1)} fusion(bf16[12,576,128]{2,1,0:T(8,128)(2,1)} %gather_fusion, pred[12]{0:T(512)(128)(4,1)S(1)} %get-tuple-element.237, pred[12]{0:T(512)(128)(4,1)S(1)} %broadcast_in_dim.122), kind=kLoop, calls=%fused_computation.28 | loop fusion | flops 1769472 | bytes 3538968 | tf_op jit(solution)/shard_map/jit(_where)/select_n | solution.py:146
  8.9 6.5 %all-to-all-start = ((bf16[12,576,128]{2,1,0:T(8,128)(2,1)}), bf16[12,576,128]{2,1,0:T(8,128)(2,1)}, u32[]{:S(2)}, u32[]{:S(2)}) async-start(bf16[12,576,128]{2,1,0:T(8,128)(2,1)} %select_select_fusion), calls=%async_computation | async-start | bytes 3538944 | tf_op jit(solution)/shard_map/all_to_all | solution.py:147
  15.4 0.2 reshape.433
  15.6 0.6 constant_dynamic-slice_fusion.3
  16.2 0.6 fusion.62
  16.8 0.2 convert_reduce_fusion
  17.0 0.2 fusion.70
  17.3 39.4 %all-to-all-done = bf16[12,576,128]{2,1,0:T(8,128)(2,1)} async-done(((bf16[12,576,128]{2,1,0:T(8,128)(2,1)}), bf16[12,576,128]{2,1,0:T(8,128)(2,1)}, u32[]{:S(2)}, u32[]{:S(2)}) %all-to-all-start) | async-done | bytes 1769504 | tf_op jit(solution)/shard_map/all_to_all | solution.py:147
  56.7 3.5 %gather_fusion.1 = bf16[12,576,128]{2,1,0:T(8,128)(2,1)} fusion(bf16[12,576,128]{2,1,0:T(8,128)(2,1)} %all-to-all-done, s32[1024]{0:T(1024)S(1)} %pad_clamp_fusion), kind=kCustom, calls=%fused_computation.1.clone | custom fusion | bytes 3538992 | tf_op jit(solution)/shard_map/jit(_take)/gather | solution.py:148
  60.2 1.7 broadcast_select_fusion
  61.9 0.8 fusion.69
  62.7 0.6 fusion.32
  63.3 2.3 %fusion.15 = f32[12,2,64,512]{3,2,1,0:T(8,128)} fusion(bf16[12,576,128]{2,1,0:T(8,128)(2,1)S(1)} %broadcast_select_fusion, f32[12,2,64,128]{3,2,1,0:T(8,128)S(1)} %get-tuple-element.233, f32[12,2,64]{2,1,0:T(2,128)S(1)} %get-tuple-element.232, s32[12]{0:T(128)S(1)} %fusion.62), kind=kOutput, calls=%fused_computation.31 | convolution fusion | flops 202113024 | bytes 5517824 | tf_op jit(solution)/shard_map/psht,pct->pshc/dot_general | solution.py:46
  65.7 0.1 multiply_reduce_fusion.1
  65.8 5.1 %all_gather.24 = bf16[4,1,2,64]{3,2,1,0:T(2,128)(2,1)S(1)} all-gather(bf16[1,1,2,64]{3,2,1,0:T(2,128)(2,1)S(1)} %fusion.52), channel_id=1, replica_groups=mesh['groups'=2,'dp'=4,'rep'=4] {'rep'}, dimensions={0}, use_global_device_ids=true | all-gather | bytes 1280 | tf_op jit(solution)/shard_map/all_gather | solution.py:18
  70.9 0.1 copy.29
  71.0 7.4 %fusion.7 = f32[2,64,1,512]{3,2,1,0:T(1,128)S(1)} fusion(f32[12,2,64,1]{0,3,2,1:T(1,128)S(1)} %copy.29, f32[12,2,64,512]{3,2,1,0:T(8,128)} %fusion.15), kind=kOutput, calls=%fused_computation.16 | convolution fusion | flops 9437184 | bytes 3414016 | tf_op jit(solution)/shard_map/jpsh,pshc->jshc/dot_general | solution.py:60
  78.4 0.2 fusion.27
  78.6 7.3 %all-gather = bf16[8,64,512]{2,1,0:T(8,128)(2,1)S(1)} all-gather(bf16[2,64,512]{2,1,0:T(8,128)(2,1)S(1)} %fusion.27), channel_id=2, replica_groups=mesh['groups'=2,'dp'=4,'rep'=4] {'rep'}, dimensions={0}, use_global_device_ids=true | all-gather | bytes 655360 | tf_op jit(solution)/shard_map/all_gather | solution.py:18
  85.9 5.1 %all_gather.23 = bf16[4,1,2,64]{3,2,1,0:T(2,128)(2,1)S(1)} all-gather(bf16[1,1,2,64]{3,2,1,0:T(2,128)(2,1)S(1)} %fusion.56), channel_id=1, replica_groups=mesh['groups'=2,'dp'=4,'rep'=4] {'rep'}, dimensions={0}, use_global_device_ids=true | all-gather | bytes 1280 | tf_op jit(solution)/shard_map/all_gather | solution.py:18
  91.0 0.6 while.19
  91.0 0.1 fusion.86
  91.3 0.1 fusion.86
  91.5 0.1 fusion.86
  91.6 0.1 copy.23
  91.7 1.0 fusion.40
  92.7 3.3 %all-to-all-start.1 = ((bf16[2,64,512]{2,0,1:T(2,128)(2,1)}), bf16[2,64,512]{2,0,1:T(2,128)(2,1)S(1)}, u32[]{:S(2)}, u32[]{:S(2)}) async-start(bf16[2,64,512]{2,0,1:T(2,128)(2,1)} %fusion.40), calls=%async_computation.1 | async-start | bytes 262144 | tf_op jit(solution)/shard_map/all_to_all | solution.py:157
  96.0 0.6 dynamic-slice
  97.2 5.2 %all-to-all-done.1 = bf16[2,64,512]{2,0,1:T(2,128)(2,1)S(1)} async-done(((bf16[2,64,512]{2,0,1:T(2,128)(2,1)}), bf16[2,64,512]{2,0,1:T(2,128)(2,1)S(1)}, u32[]{:S(2)}, u32[]{:S(2)}) %all-to-all-start.1) | async-done | bytes 131104 | tf_op jit(solution)/shard_map/all_to_all | solution.py:157
  102.5 0.1 copy.40
  102.6 4.4 %convolution_convert_fusion.3 = bf16[8,1792]{1,0:T(8,128)(2,1)S(1)} fusion(bf16[2048,1792]{1,0:T(8,128)(2,1)} %param.24, bf16[8,16,512]{2,0,1:T(8,128)(2,1)S(1)} %all_to_all.20, bf16[16,512,128]{2,1,0:T(8,128)(2,1)S(1)} %copy-done), kind=kOutput, calls=%fused_computation.23 | convolution fusion | flops 75528192 | bytes 9596928 | tf_op jit(solution)/shard_map/dot_general | solution.py:162
  107.1 17.5 %all-reduce = bf16[8,1792]{1,0:T(8,128)(2,1)S(1)} all-reduce(bf16[8,1792]{1,0:T(8,128)(2,1)S(1)} %convolution_convert_fusion.3), channel_id=3, replica_groups=mesh['groups'=2,'dp'=4,'rep'=4] {'dp'}, use_global_device_ids=true, to_apply=%region_12.14.clone | all-reduce | flops 14336 | bytes 57344
  124.5 0.1 multiply_reduce_fusion
  124.7 5.7 %psum.7 = f32[2]{0:T(128)S(1)} all-reduce(f32[2]{0:T(128)S(1)} %multiply_reduce_fusion), channel_id=1, replica_groups=mesh['groups'=2,'dp'=4,'rep'=4] {'rep'}, use_global_device_ids=true, to_apply=%region_14.16 | all-reduce | flops 2 | bytes 16 | tf_op jit(solution)/shard_map/psum | solution.py:168
  130.4 13.4 %all-gather.1 = bf16[4,2,1792]{2,1,0:T(2,128)(2,1)S(1)} all-gather(bf16[1,2,1792]{2,1,0:T(2,128)(2,1)S(1)} %fusion.45), channel_id=1, replica_groups=mesh['groups'=2,'dp'=4,'rep'=4] {'dp'}, dimensions={0}, use_global_device_ids=true | all-gather | bytes 35840 | tf_op jit(solution)/shard_map/all_gather | solution.py:172
  143.8 5.7 %fusion.10 = bf16[1,8,3072]{2,1,0:T(8,128)(2,1)S(1)} fusion(bf16[8,1792]{1,0:T(8,128)(2,1)S(1)} %reshape.464, bf16[1792,3072]{1,0:T(8,128)(2,1)} %param.28), kind=kOutput, calls=%fused_computation.21 | convolution fusion | flops 88104960 | bytes 11087872 | tf_op jit(solution)/shard_map/dot_general | solution.py:174
  149.5 5.7 %fusion.9 = bf16[1,8,3072]{2,1,0:T(8,128)(2,1)S(1)} fusion(bf16[8,1792]{1,0:T(8,128)(2,1)S(1)} %reshape.464, bf16[1792,3072]{1,0:T(8,128)(2,1)} %param.27), kind=kOutput, calls=%fused_computation.20 | convolution fusion | flops 88104960 | bytes 11087872 | tf_op jit(solution)/shard_map/dot_general | solution.py:173
  155.1 6.7 %all_gather.26 = bf16[4,8,6144]{2,1,0:T(8,128)(2,1)S(1)} all-gather(bf16[1,8,6144]{2,1,0:T(8,128)(2,1)S(1)} %pad_maximum_fusion), channel_id=1, replica_groups=mesh['groups'=2,'dp'=4,'rep'=4] {'rep'}, dimensions={0}, use_global_device_ids=true | all-gather | bytes 491520 | tf_op jit(solution)/shard_map/all_gather | solution.py:176
  161.9 5.7 %convolution_convert_fusion.2 = bf16[8,1792]{1,0:T(8,128)(2,1)S(1)} fusion(bf16[3072,1792]{1,0:T(8,128)(2,1)} %param.29, f32[8,6144]{1,0:T(8,128)S(1)} %convert_element_type.212), kind=kOutput, calls=%fused_computation.22 | convolution fusion | flops 88242176 | bytes 11235328 | tf_op jit(solution)/shard_map/dot_general | solution.py:185
  167.6 15.9 %all-reduce.1 = bf16[8,1792]{1,0:T(8,128)(2,1)S(1)} all-reduce(bf16[8,1792]{1,0:T(8,128)(2,1)S(1)} %convolution_convert_fusion.2), channel_id=4, replica_groups=mesh['groups'=2,'dp'=4,'rep'=4] {'dp'}, use_global_device_ids=true, to_apply=%region_16.18.clone | all-reduce | flops 14336 | bytes 57344
  183.4 0.6 add_convert_fusion
  (49 shorter events, 0.8 us)
Async XLA Ops:
  0.0 102.6 %copy-start = (bf16[16,512,128]{2,1,0:T(8,128)(2,1)S(1)}, bf16[16,512,128]{2,1,0:T(8,128)(2,1)}, u32[]{:S(2)}) copy-start(bf16[16,512,128]{2,1,0:T(8,128)(2,1)} %param.23) | copy-start | bytes 6291460
  8.9 6.5 %copy-start.1 = (bf16[2,36864]{1,0:T(2,128)(2,1)S(1)}, bf16[2,36864]{1,0:T(2,128)(2,1)}, u32[]{:S(2)}) copy-start(bf16[2,36864]{1,0:T(2,128)(2,1)} %param.21) | copy-start | bytes 442372
  8.9 6.7 %copy-start.6 = (s32[4,1]{0,1:T(1,128)S(1)}, s32[4,1]{0,1:T(1,128)}, u32[]{:S(2)}) copy-start(s32[4,1]{0,1:T(1,128)} %param.20) | copy-start | bytes 52
  8.9 7.3 %copy-start.5 = (s32[4,12]{1,0:T(4,128)S(1)}, s32[4,12]{1,0:T(4,128)}, u32[]{:S(2)}) copy-start(s32[4,12]{1,0:T(4,128)} %param.18) | copy-start | bytes 580
  8.9 8.1 %copy-start.3 = (bf16[2,576]{1,0:T(2,128)(2,1)S(1)}, bf16[2,576]{1,0:T(2,128)(2,1)}, u32[]{:S(2)}) copy-start(bf16[2,576]{1,0:T(2,128)(2,1)} %param.22) | copy-start | bytes 6916
  8.9 47.8 %all-to-all-start = ((bf16[12,576,128]{2,1,0:T(8,128)(2,1)}), bf16[12,576,128]{2,1,0:T(8,128)(2,1)}, u32[]{:S(2)}, u32[]{:S(2)}) async-start(bf16[12,576,128]{2,1,0:T(8,128)(2,1)} %select_select_fusion), calls=%async_computation | async-start | bytes 3538944 | tf_op jit(solution)/shard_map/all_to_all | solution.py:147
  91.0 5.0 %copy-start.7 = (u32[32]{0:T(128)S(1)}, u32[32]{0:T(128)}, u32[]{:S(2)}) copy-start(u32[32]{0:T(128)} %constant.151) | copy-start | bytes 388
  92.7 9.8 %all-to-all-start.1 = ((bf16[2,64,512]{2,0,1:T(2,128)(2,1)}), bf16[2,64,512]{2,0,1:T(2,128)(2,1)S(1)}, u32[]{:S(2)}, u32[]{:S(2)}) async-start(bf16[2,64,512]{2,0,1:T(2,128)(2,1)} %fusion.40), calls=%async_computation.1 | async-start | bytes 262144 | tf_op jit(solution)/shard_map/all_to_all | solution.py:157
  102.6 21.9 %copy-start.2 = (bf16[2,1792]{1,0:T(2,128)(2,1)S(1)}, bf16[2,1792]{1,0:T(2,128)(2,1)}, u32[]{:S(2)}) copy-start(bf16[2,1792]{1,0:T(2,128)(2,1)} %param.25) | copy-start | bytes 21508
  102.6 27.7 %copy-start.4 = (f32[1792]{0:T(1024)S(1)}, f32[1792]{0:T(1024)}, u32[]{:S(2)}) copy-start(f32[1792]{0:T(1024)} %param.26) | copy-start | bytes 21508
